TPU v7x, 512 devices: a whole 4x4x16 slice. The times are simulated.
512 devices in a mesh: rep: 4 (over x), fsdp: 16 (over z), tp: 8 (over y, core).
Axes of the slice: x: 4, y: 4, z: 16, core: 2. Of those that a mesh axis runs over, the one named last changes fastest.
Arguments:
- tracker: bfloat16 [4, 4096, 14336], P('rep', 'fsdp', 'tp'), may hold values from -20 to 20
- grad_delta: bfloat16 [4, 4096, 14336], P('rep', 'fsdp', 'tp'), may hold values from -20 to 20
- momentum: bfloat16 [4, 4096, 14336], P('rep', 'fsdp', 'tp'), may hold values from -20 to 20
- q_basis: bfloat16 [4, 14336, 512], P('rep', 'tp', 'fsdp'), may hold values from -0.046875 to 0.046875
- mix_counts: int32 [4, 3], replicated, may hold values from 1 to 8
Outputs:
- new_tracker: bfloat16 [4, 4096, 14336], P('rep', 'fsdp', 'tp')
- new_momentum: bfloat16 [4, 4096, 14336], P('rep', 'fsdp', 'tp')
- left_basis: bfloat16 [4, 4096, 512], P('rep', 'fsdp')
- q_new: bfloat16 [4, 14336, 512], P('rep', 'tp', 'fsdp')
All inputs are finite; a program needn't handle non-finite values.
Results may differ from a plain program's by a relative error of at most 0.0061.
Values may be sent and summed in bfloat16 or wider, within the bound.
A program may use at most 64 MiB of HBM per device.

v0:
```python
import jax
import jax.numpy as jnp
from jax import lax
from jax.sharding import PartitionSpec as P

D = 4096
FF = 14336


def extended(block, sides, width):
    for axis, dim in sides:
        count = lax.axis_size(axis)
        forward = [(i, i + 1) for i in range(count - 1)]
        forward.append((count - 1, 0))
        backward = [(target, source) for source, target in forward]
        low = lax.ppermute(
            lax.slice_in_dim(block, block.shape[dim] - width, None, axis=dim), axis, forward
        )
        high = lax.ppermute(lax.slice_in_dim(block, 0, width, axis=dim), axis, backward)
        block = jnp.concatenate([low, block, high], axis=dim)
    return block


def orthonormal(pmat, gram):
    factor = jnp.linalg.cholesky(gram)
    solved = jax.scipy.linalg.solve_triangular(factor, pmat.T, lower=True).T
    return (solved * jnp.sqrt(jnp.float32(D))).astype(jnp.bfloat16)


def local(tracker, grad_delta, momentum, q_basis, mix_counts):
    agent = lax.axis_index("rep")
    counts = mix_counts.astype(jnp.float32)
    select = (jnp.arange(counts.shape[0]) == agent).astype(jnp.float32)
    mine = jnp.sum(select[:, None] * counts, axis=0)
    weights = mine / jnp.sum(mine)
    near = extended(tracker, (("rep", 0),), 1)
    mixed = (
        weights[0] * near[1].astype(jnp.float32)
        + weights[1] * near[0].astype(jnp.float32)
        + weights[2] * near[2].astype(jnp.float32)
    )
    tracked = mixed + grad_delta[0].astype(jnp.float32)
    new_tracker = tracked.astype(jnp.bfloat16)
    accum = momentum[0].astype(jnp.float32) + tracked
    accum_b = accum.astype(jnp.bfloat16)
    scale = 1.0 / jnp.sqrt(jnp.float32(D))
    basis_full = lax.all_gather(q_basis, "fsdp", axis=2, tiled=True)[0]
    partial_left = jnp.dot(accum_b, basis_full, preferred_element_type=jnp.float32)
    pmat = lax.psum(partial_left, "tp")
    gram_part = jnp.dot(pmat.T, pmat, precision=lax.Precision.HIGHEST)
    gram = lax.psum(gram_part, "fsdp")
    left_b = orthonormal(pmat, gram)
    block = left_b
    product = lax.dot_general(
        block, accum_b, (((0,), (0,)), ((), ())), preferred_element_type=jnp.float32
    )
    right_t = lax.psum_scatter(product * scale, "fsdp", scatter_dimension=0, tiled=True)
    squares = lax.psum(jnp.sum(right_t * right_t, axis=1), "tp")
    rms = jnp.sqrt(squares / FF) + 1e-06
    q_new = (right_t / rms[:, None]).T.astype(jnp.bfloat16)
    right_b = right_t.astype(jnp.bfloat16)
    block = left_b
    feed = jnp.dot(
        block,
        lax.all_gather(right_b, "fsdp", axis=0, tiled=True),
        preferred_element_type=jnp.float32,
    )
    new_momentum = (accum - 0.5 * scale * feed).astype(jnp.bfloat16)
    return (new_tracker[None], new_momentum[None], left_b[None], q_new[None])


def solution(mesh):
    in_specs = (
        P("rep", "fsdp", "tp"),
        P("rep", "fsdp", "tp"),
        P("rep", "fsdp", "tp"),
        P("rep", "tp", "fsdp"),
        P(),
    )
    out_specs = (
        P("rep", "fsdp", "tp"),
        P("rep", "fsdp", "tp"),
        P("rep", "fsdp", None),
        P("rep", "tp", "fsdp"),
    )
    return jax.shard_map(local, mesh=mesh, in_specs=in_specs, out_specs=out_specs, check_vma=False)
```

profile of v0, /device:TPU:2, one launch (start us, length us, event | category | flops | bytes accessed | tf_op | source)
XLA Modules:
  0.0 640.5 jit_solution(14598845073682928262)
XLA Ops:
  7.9 7.8 %collective-permute-start.1 = (bf16[1,256,1792]{2,1,0:T(8,128)(2,1)}, bf16[1,256,1792]{2,1,0:T(8,128)(2,1)S(1)}, u32[]{:S(2)}, u32[]{:S(2)}) collective-permute-start(bf16[1,256,1792]{2,1,0:T(8,128)(2,1)} %param.5), channel_id=1, source_target_pairs={{128,0},{256,128},{384,256},{0,384},{129,1},{257,129},{385,257},{1... | collective-permute-start | bytes 2752520 | tf_op jit(solution)/shard_map/ppermute | solution.py:19
  20.3 11.8 %collective-permute-done.1 = bf16[1,256,1792]{2,1,0:T(8,128)(2,1)S(1)} collective-permute-done((bf16[1,256,1792]{2,1,0:T(8,128)(2,1)}, bf16[1,256,1792]{2,1,0:T(8,128)(2,1)S(1)}, u32[]{:S(2)}, u32[]{:S(2)}) %collective-permute-start.1) | collective-permute-done | bytes 917536 | tf_op jit(solution)/shard_map/ppermute | solution.py:19
  32.1 3.2 collective-permute-done
  36.3 5.5 fusion.44
  41.8 45.7 %all-gather.3.cloned.1.call-done = bf16[1,1792,512]{1,2,0:T(8,128)(2,1)} async-done(((bf16[1,1792,32]{1,2,0:T(8,128)(2,1)}), bf16[1,1792,512]{1,2,0:T(8,128)(2,1)}) %all-gather.3.cloned.1.call-update) | async-done | bytes 1835024 | tf_op jit(solution)/shard_map/all_gather | solution.py:47
  87.5 3.0 fusion.3
  90.6 73.0 %all-reduce.4.cloned.1.call-done = f32[256,512]{1,0:T(8,128)} async-done(((f32[256,512]{1,0:T(8,128)}), f32[256,512]{1,0:T(8,128)}) %all-reduce.4.cloned.1.call-update) | async-done | bytes 524304 | tf_op jit(solution)/shard_map/psum | solution.py:49
  163.6 3.3 fusion.47
  167.1 138.0 %all-reduce.6.cloned.1.call-done = f32[512,512]{0,1:T(8,128)} async-done(((f32[512,512]{0,1:T(8,128)}), f32[512,512]{0,1:T(8,128)}) %all-reduce.6.cloned.1.call-update) | async-done | bytes 1048592 | tf_op jit(solution)/shard_map/psum | solution.py:51
  310.5 11.7 %cholesky.104 = f32[128,128]{1,0:T(8,128)S(1)} custom-call(f32[128,128]{1,0:T(8,128)S(1)} %cholesky.266), custom_call_target="Cholesky" | custom-call | tf_op jit(solution)/shard_map/jit(cholesky)/cholesky | solution.py:25
  323.4 9.8 %custom-call.31 = f32[1,128,128]{1,2,0:T(8,128)S(1)} custom-call(f32[1,128,128]{2,1,0:T(8,128)S(1)} %get-tuple-element.41), custom_call_target="InvertDiagBlocksLowerTriangular" | custom-call | tf_op jit(solution)/shard_map/jit(cholesky)/cholesky | solution.py:25
  336.5 11.7 %cholesky.217 = f32[128,128]{1,0:T(8,128)S(1)} custom-call(f32[128,128]{1,0:T(8,128)S(1)} %cholesky.270), custom_call_target="Cholesky" | custom-call | tf_op jit(solution)/shard_map/jit(cholesky)/cholesky | solution.py:25
  348.8 10.0 %custom-call.32 = f32[1,128,128]{1,2,0:T(8,128)S(1)} custom-call(f32[1,128,128]{2,1,0:T(8,128)S(1)} %get-tuple-element.38), custom_call_target="InvertDiagBlocksLowerTriangular" | custom-call | tf_op jit(solution)/shard_map/jit(cholesky)/cholesky | solution.py:25
  361.2 11.7 %cholesky.238 = f32[128,128]{1,0:T(8,128)S(1)} custom-call(f32[128,128]{1,0:T(8,128)S(1)} %cholesky.275), custom_call_target="Cholesky" | custom-call | tf_op jit(solution)/shard_map/jit(cholesky)/cholesky | solution.py:25
  373.6 9.8 %custom-call.33 = f32[1,128,128]{1,2,0:T(8,128)S(1)} custom-call(f32[1,128,128]{2,1,0:T(8,128)S(1)} %get-tuple-element.35), custom_call_target="InvertDiagBlocksLowerTriangular" | custom-call | tf_op jit(solution)/shard_map/jit(cholesky)/cholesky | solution.py:25
  385.6 11.7 %cholesky.255 = f32[128,128]{1,0:T(8,128)S(1)} custom-call(f32[128,128]{1,0:T(8,128)S(1)} %convolution_subtract_fusion.5), custom_call_target="Cholesky" | custom-call | tf_op jit(solution)/shard_map/jit(cholesky)/cholesky | solution.py:25
  405.1 14.5 %while.1 = (s32[]{:T(128)}, f32[512,512]{1,0:T(8,128)}, s32[4,2]{0,1:T(2,128)S(1)}, f32[4,128,128]{2,1,0:T(8,128)}, s32[]{:T(128)}) while((s32[]{:T(128)}, f32[512,512]{1,0:T(8,128)}, s32[4,2]{0,1:T(2,128)S(1)}, f32[4,128,128]{2,1,0:T(8,128)}, s32[]{:T(128)}) %tuple.37), condition=%wide.while_cond, body=%wide.while_body.sunk | while | flops 2 | bytes 132205 | solution.py:26
  405.8 3.0 bitcast_dynamic-update-slice_fusion.2
  413.1 3.0 bitcast_dynamic-update-slice_fusion.2
  419.6 40.8 %custom-call.34 = f32[4,128,128]{1,2,0:T(8,128)} custom-call(f32[4,128,128]{2,1,0:T(8,128)} %get-tuple-element.11), custom_call_target="InvertDiagBlocksLowerTriangular" | custom-call | tf_op jit(solution)/shard_map/jit(_solve_triangular)/triangular_solve | solution.py:26
  472.1 75.2 %reduce-scatter.2.cloned.1.call-done = f32[32,1792]{1,0:T(8,128)} async-done(((f32[512,1792]{1,0:T(8,128)}), f32[32,1792]{1,0:T(8,128)}) %reduce-scatter.2.cloned.1.call-update) | async-done | bytes 229392 | tf_op jit(solution)/shard_map/reduce_scatter | solution.py:57
  548.4 12.4 %psum.23 = f32[32]{0:T(128)S(1)} all-reduce(f32[32]{0:T(128)S(1)} %multiply_reduce_fusion), channel_id=1, replica_groups=mesh['rep'=4,'fsdp'=16,'tp'=8] {'tp'}, use_global_device_ids=true, to_apply=%region_14.15 | all-reduce | flops 32 | bytes 256 | tf_op jit(solution)/shard_map/psum | solution.py:58
  563.5 67.4 %all-gather.5.cloned.1.call-done = bf16[512,1792]{1,0:T(8,128)(2,1)} async-done(((bf16[32,1792]{1,0:T(8,128)(2,1)}), bf16[512,1792]{1,0:T(8,128)(2,1)}) %all-gather.5.cloned.1.call-update) | async-done | bytes 1835024 | tf_op jit(solution)/shard_map/all_gather | solution.py:65
  630.9 3.1 fusion.2
  (75 shorter events, 51.4 us)
Async XLA Ops:
  7.2 80.3 %all-gather.3.cloned.1.call-start = ((), (), s32[]{:S(2)}) async-start(), calls=%async_computation.1 | async-start | bytes 1949696 | tf_op jit(solution)/shard_map/all_gather | solution.py:47
  7.9 155.7 %all-reduce.4.cloned.1.call-start = ((), (), s32[]{:S(2)}) async-start(), calls=%async_computation.2 | async-start | bytes 1048576 | tf_op jit(solution)/shard_map/psum | solution.py:49
  7.9 24.2 %collective-permute-start.1 = (bf16[1,256,1792]{2,1,0:T(8,128)(2,1)}, bf16[1,256,1792]{2,1,0:T(8,128)(2,1)S(1)}, u32[]{:S(2)}, u32[]{:S(2)}) collective-permute-start(bf16[1,256,1792]{2,1,0:T(8,128)(2,1)} %param.5), channel_id=1, source_target_pairs={{128,0},{256,128},{384,256},{0,384},{129,1},{257,129},{385,257},{1... | collective-permute-start | bytes 2752520 | tf_op jit(solution)/shard_map/ppermute | solution.py:19
  15.8 19.6 %collective-permute-start = (bf16[1,256,1792]{2,1,0:T(8,128)(2,1)}, bf16[1,256,1792]{2,1,0:T(8,128)(2,1)S(1)}, u32[]{:S(2)}, u32[]{:S(2)}) collective-permute-start(bf16[1,256,1792]{2,1,0:T(8,128)(2,1)} %param.5), channel_id=1, source_target_pairs={{0,128},{128,256},{256,384},{384,0},{1,129},{129,257},{257,385},{3... | collective-permute-start | bytes 2752520 | tf_op jit(solution)/shard_map/ppermute | solution.py:16
  32.1 3.2 copy-start.5
  35.3 0.9 copy-start.6
  36.3 51.2 %copy-start = (bf16[1,256,1792]{2,1,0:T(8,128)(2,1)S(1)}, bf16[1,256,1792]{2,1,0:T(8,128)(2,1)}, u32[]{:S(2)}) copy-start(bf16[1,256,1792]{2,1,0:T(8,128)(2,1)} %param.7) | copy-start | bytes 2752516
  90.5 214.6 %all-reduce.6.cloned.1.call-start = ((), (), s32[]{:S(2)}) async-start(), calls=%async_computation.3 | async-start | bytes 2097152 | tf_op jit(solution)/shard_map/psum | solution.py:51
  166.9 380.4 %reduce-scatter.2.cloned.1.call-start = ((), (), s32[]{:S(2)}) async-start(), calls=%async_computation.4 | async-start | bytes 3899392 | tf_op jit(solution)/shard_map/reduce_scatter | solution.py:57
  309.5 1.0 copy-start.4
  373.6 86.8 %copy-start.1 = (f32[256,512]{1,0:T(8,128)S(1)}, f32[256,512]{1,0:T(8,128)}, u32[]{:S(2)}) copy-start(f32[256,512]{1,0:T(8,128)} %all-reduce.4.cloned.1.call-done) | copy-start | bytes 1572868
  466.6 3.0 copy-start.2
  472.0 90.6 %copy-start.3 = (f32[128,256]{1,0:T(8,128)S(1)}, f32[128,256]{1,0:T(8,128)}, u32[]{:S(2)}) copy-start(f32[128,256]{1,0:T(8,128)} %copy-done.2) | copy-start | bytes 393220
  472.1 158.8 %all-gather.5.cloned.1.call-start = ((), (), s32[]{:S(2)}) async-start(), calls=%async_computation.5 | async-start | bytes 1949696 | tf_op jit(solution)/shard_map/all_gather | solution.py:65
Sparse Core Ops, SparseCore 0:
  10.1 77.3 all-gather.2
  90.6 72.8 all-reduce.3
  167.0 138.0 all-reduce.5
  472.2 75.0 reduce-scatter.1
  562.7 68.1 all-gather.4
where the time goes:
time: 642 us; the launch traced here: 641 us
  waiting for transfers between devices  415 us (65%)
  other arithmetic  136 us (21%)
  matrix products  28.8 us (4%)
  local copies, waits for them, and re-layouts  21.6 us (3%)
  between operations  16.5 us (3%)
  blocking collectives  12.4 us (2%)
  starting transfers between devices  10.1 us (2%)
    psum x1, waiting for transfers between devices, local(): gram = lax.psum(gram_part, 'fsdp')  138 us
    another operation x14, other arithmetic, orthonormal(): factor = jnp.linalg.cholesky(gram)  80.4 us
    reduce_scatter x1, waiting for transfers between devices, local(): lax.psum_scatter(product * scale, 'fsdp', scatter_dimension=0, tiled=True)  75.2 us
    psum x1, waiting for transfers between devices, local(): pmat = lax.psum(partial_left, 'tp')  73 us
    all_gather x1, waiting for transfers between devices, local(): lax.all_gather(right_b, 'fsdp', axis=0, tiled=True)  67.4 us
    all_gather x1, waiting for transfers between devices, local(): basis_full = lax.all_gather(q_basis, 'fsdp', axis=2, tiled=True)[0]  45.7 us
    another operation x3, other arithmetic, orthonormal(): solved = jax.scipy.linalg.solve_triangular(factor, pmat.T, lower=True).T  43.4 us
    another operation x12, local copies, waits for them, and re-layouts  14.5 us
  transfers between devices with their start and end apart: 7, of which 7 were waited for; matrix products, arithmetic and copies ran while one was open for 1% of the time, Pallas kernels for 0%

commit v1 on v0

--- a/solution.py
+++ b/solution.py
@@ -44,7 +44,9 @@
     accum = momentum[0].astype(jnp.float32) + tracked
     accum_b = accum.astype(jnp.bfloat16)
     scale = 1.0 / jnp.sqrt(jnp.float32(D))
-    basis_full = lax.all_gather(q_basis, "fsdp", axis=2, tiled=True)[0]
+    basis_full = jnp.concatenate(
+        lax.all_to_all(jnp.stack([q_basis] * lax.axis_size("fsdp")), "fsdp", 0, 0), axis=2
+    )[0]
     partial_left = jnp.dot(accum_b, basis_full, preferred_element_type=jnp.float32)
     pmat = lax.psum(partial_left, "tp")
     gram_part = jnp.dot(pmat.T, pmat, precision=lax.Precision.HIGHEST)

time: 642 us -> 664 us (1.034)
  starting transfers between devices: 10.1 us -> 21.6 us
  waiting for transfers between devices: 415 us -> 424 us
    all_to_all x0 -> x1, waiting for transfers between devices: none -> 51.9 us  [local(): lax.all_to_all(jnp.stack([q_basis] * lax.axis_size('fsdp')), 'fsdp', 0, 0)]
    all_gather x1 -> x0, waiting for transfers between devices: 45.7 us -> none  [local(): basis_full = lax.all_gather(q_basis, 'fsdp', axis=2, tiled=True)[0]]
    all_to_all x0 -> x1, starting transfers between devices: none -> 15.4 us  [local(): lax.all_to_all(jnp.stack([q_basis] * lax.axis_size('fsdp')), 'fsdp', 0, 0)]
    another operation x12 -> x13, local copies, waits for them, and re-layouts: 14.5 us -> 16.8 us
where the time goes in v1:
time: 664 us; the launch traced here: 662 us
  waiting for transfers between devices  424 us (64%)
  other arithmetic  135 us (20%)
  matrix products  28.8 us (4%)
  local copies, waits for them, and re-layouts  23.9 us (4%)
  starting transfers between devices  21.6 us (3%)
  between operations  16.5 us (2%)
  blocking collectives  12.4 us (2%)
    psum x1, waiting for transfers between devices, local(): gram = lax.psum(gram_part, 'fsdp')  138 us
    another operation x14, other arithmetic, orthonormal(): factor = jnp.linalg.cholesky(gram)  80.4 us
    reduce_scatter x1, waiting for transfers between devices, local(): lax.psum_scatter(product * scale, 'fsdp', scatter_dimension=0, tiled=True)  75 us
    psum x1, waiting for transfers between devices, local(): pmat = lax.psum(partial_left, 'tp')  72 us
    all_gather x1, waiting for transfers between devices, local(): lax.all_gather(right_b, 'fsdp', axis=0, tiled=True)  67.9 us
    all_to_all x1, waiting for transfers between devices, local(): lax.all_to_all(jnp.stack([q_basis] * lax.axis_size('fsdp')), 'fsdp', 0, 0)  51.9 us
    another operation x3, other arithmetic, orthonormal(): solved = jax.scipy.linalg.solve_triangular(factor, pmat.T, lower=True).T  43.4 us
    ppermute x1, waiting for transfers between devices, extended(): lax.ppermute(lax.slice_in_dim(block, 0, width, axis=dim), axis, backward)  15.9 us
  transfers between devices with their start and end apart: 7, of which 7 were waited for; matrix products, arithmetic and copies ran while one was open for 1% of the time, Pallas kernels for 0%

profile of v1, /device:TPU:2, one launch (start us, length us, event | category | flops | bytes accessed | tf_op | source)
XLA Modules:
  0.0 662.4 jit_solution(8581217549100627083)
XLA Ops:
  9.5 15.4 %all-to-all-start = ((bf16[16,1,1792,32]{2,3,1,0:T(8,128)(2,1)}), bf16[16,1,1792,32]{2,3,1,0:T(8,128)(2,1)}, u32[]{:S(2)}, u32[]{:S(2)}) async-start(bf16[16,1,1792,32]{2,3,1,0:T(8,128)(2,1)} %stack.2), calls=%async_computation | async-start | bytes 3670016 | tf_op jit(solution)/shard_map/all_to_all | solution.py:48
  27.4 3.4 collective-permute-start
  32.7 15.9 %collective-permute-done.1 = bf16[1,256,1792]{2,1,0:T(8,128)(2,1)S(1)} collective-permute-done((bf16[1,256,1792]{2,1,0:T(8,128)(2,1)S(1)}, bf16[1,256,1792]{2,1,0:T(8,128)(2,1)S(1)}, u32[]{:S(2)}, u32[]{:S(2)}) %collective-permute-start.1) | collective-permute-done | bytes 917536 | tf_op jit(solution)/shard_map/ppermute | solution.py:19
  48.6 3.2 collective-permute-done
  52.7 5.5 fusion.43
  58.2 51.9 %all-to-all-done = bf16[16,1,1792,32]{2,3,1,0:T(8,128)(2,1)} async-done(((bf16[16,1,1792,32]{2,3,1,0:T(8,128)(2,1)}), bf16[16,1,1792,32]{2,3,1,0:T(8,128)(2,1)}, u32[]{:S(2)}, u32[]{:S(2)}) %all-to-all-start) | async-done | bytes 1835040 | tf_op jit(solution)/shard_map/all_to_all | solution.py:48
  110.1 3.0 fusion.4
  113.2 72.0 %all-reduce.4.cloned.1.call-done = f32[256,512]{1,0:T(8,128)} async-done(((f32[256,512]{1,0:T(8,128)}), f32[256,512]{1,0:T(8,128)}) %all-reduce.4.cloned.1.call-update) | async-done | bytes 524304 | tf_op jit(solution)/shard_map/psum | solution.py:51
  185.1 3.3 fusion.46
  188.7 138.0 %all-reduce.6.cloned.1.call-done = f32[512,512]{0,1:T(8,128)} async-done(((f32[512,512]{0,1:T(8,128)}), f32[512,512]{0,1:T(8,128)}) %all-reduce.6.cloned.1.call-update) | async-done | bytes 1048592 | tf_op jit(solution)/shard_map/psum | solution.py:53
  332.1 11.7 %cholesky.104 = f32[128,128]{1,0:T(8,128)S(1)} custom-call(f32[128,128]{1,0:T(8,128)S(1)} %cholesky.266), custom_call_target="Cholesky" | custom-call | tf_op jit(solution)/shard_map/jit(cholesky)/cholesky | solution.py:25
  345.0 9.8 %custom-call.31 = f32[1,128,128]{1,2,0:T(8,128)S(1)} custom-call(f32[1,128,128]{2,1,0:T(8,128)S(1)} %get-tuple-element.49), custom_call_target="InvertDiagBlocksLowerTriangular" | custom-call | tf_op jit(solution)/shard_map/jit(cholesky)/cholesky | solution.py:25
  358.0 11.7 %cholesky.217 = f32[128,128]{1,0:T(8,128)S(1)} custom-call(f32[128,128]{1,0:T(8,128)S(1)} %cholesky.270), custom_call_target="Cholesky" | custom-call | tf_op jit(solution)/shard_map/jit(cholesky)/cholesky | solution.py:25
  370.4 10.0 %custom-call.32 = f32[1,128,128]{1,2,0:T(8,128)S(1)} custom-call(f32[1,128,128]{2,1,0:T(8,128)S(1)} %get-tuple-element.46), custom_call_target="InvertDiagBlocksLowerTriangular" | custom-call | tf_op jit(solution)/shard_map/jit(cholesky)/cholesky | solution.py:25
  382.8 11.7 %cholesky.238 = f32[128,128]{1,0:T(8,128)S(1)} custom-call(f32[128,128]{1,0:T(8,128)S(1)} %cholesky.275), custom_call_target="Cholesky" | custom-call | tf_op jit(solution)/shard_map/jit(cholesky)/cholesky | solution.py:25
  395.1 9.8 %custom-call.33 = f32[1,128,128]{1,2,0:T(8,128)S(1)} custom-call(f32[1,128,128]{2,1,0:T(8,128)S(1)} %get-tuple-element.43), custom_call_target="InvertDiagBlocksLowerTriangular" | custom-call | tf_op jit(solution)/shard_map/jit(cholesky)/cholesky | solution.py:25
  407.2 11.7 %cholesky.255 = f32[128,128]{1,0:T(8,128)S(1)} custom-call(f32[128,128]{1,0:T(8,128)S(1)} %convolution_subtract_fusion.5), custom_call_target="Cholesky" | custom-call | tf_op jit(solution)/shard_map/jit(cholesky)/cholesky | solution.py:25
  426.7 14.5 %while.1 = (s32[]{:T(128)}, f32[512,512]{1,0:T(8,128)}, s32[4,2]{0,1:T(2,128)S(1)}, f32[4,128,128]{2,1,0:T(8,128)}, s32[]{:T(128)}) while((s32[]{:T(128)}, f32[512,512]{1,0:T(8,128)}, s32[4,2]{0,1:T(2,128)S(1)}, f32[4,128,128]{2,1,0:T(8,128)}, s32[]{:T(128)}) %tuple.39), condition=%wide.while_cond, body=%wide.while_body.sunk | while | flops 2 | bytes 132205 | solution.py:26
  427.4 3.0 bitcast_dynamic-update-slice_fusion.2
  441.2 40.8 %custom-call.34 = f32[4,128,128]{1,2,0:T(8,128)} custom-call(f32[4,128,128]{2,1,0:T(8,128)} %get-tuple-element.11), custom_call_target="InvertDiagBlocksLowerTriangular" | custom-call | tf_op jit(solution)/shard_map/jit(_solve_triangular)/triangular_solve | solution.py:26
  493.7 75.0 %reduce-scatter.2.cloned.1.call-done = f32[32,1792]{1,0:T(8,128)} async-done(((f32[512,1792]{1,0:T(8,128)}), f32[32,1792]{1,0:T(8,128)}) %reduce-scatter.2.cloned.1.call-update) | async-done | bytes 229392 | tf_op jit(solution)/shard_map/reduce_scatter | solution.py:59
  569.7 12.4 %psum.23 = f32[32]{0:T(128)S(1)} all-reduce(f32[32]{0:T(128)S(1)} %multiply_reduce_fusion), channel_id=1, replica_groups=mesh['rep'=4,'fsdp'=16,'tp'=8] {'tp'}, use_global_device_ids=true, to_apply=%region_14.15 | all-reduce | flops 32 | bytes 256 | tf_op jit(solution)/shard_map/psum | solution.py:60
  584.9 67.9 %all-gather.2.cloned.1.call-done = bf16[512,1792]{1,0:T(8,128)(2,1)} async-done(((bf16[32,1792]{1,0:T(8,128)(2,1)}), bf16[512,1792]{1,0:T(8,128)(2,1)}) %all-gather.2.cloned.1.call-update) | async-done | bytes 1835024 | tf_op jit(solution)/shard_map/all_gather | solution.py:67
  652.8 3.1 fusion.2
  (79 shorter events, 55.8 us)
Async XLA Ops:
  9.5 15.4 %copy-start.5 = (bf16[1,256,1792]{2,1,0:T(8,128)(2,1)S(1)}, bf16[1,256,1792]{2,1,0:T(8,128)(2,1)}, u32[]{:S(2)}) copy-start(bf16[1,256,1792]{2,1,0:T(8,128)(2,1)} %param.5) | copy-start | bytes 2752516
  9.5 21.3 %copy-start.8 = (s32[4,3]{1,0:T(4,128)S(1)}, s32[4,3]{1,0:T(4,128)}, u32[]{:S(2)}) copy-start(s32[4,3]{1,0:T(4,128)} %param.9) | copy-start | bytes 148
  9.5 100.6 %all-to-all-start = ((bf16[16,1,1792,32]{2,3,1,0:T(8,128)(2,1)}), bf16[16,1,1792,32]{2,3,1,0:T(8,128)(2,1)}, u32[]{:S(2)}, u32[]{:S(2)}) async-start(bf16[16,1,1792,32]{2,3,1,0:T(8,128)(2,1)} %stack.2), calls=%async_computation | async-start | bytes 3670016 | tf_op jit(solution)/shard_map/all_to_all | solution.py:48
  24.9 160.3 %all-reduce.4.cloned.1.call-start = ((), (), s32[]{:S(2)}) async-start(), calls=%async_computation.2 | async-start | bytes 1048576 | tf_op jit(solution)/shard_map/psum | solution.py:51
  24.9 23.7 %collective-permute-start.1 = (bf16[1,256,1792]{2,1,0:T(8,128)(2,1)S(1)}, bf16[1,256,1792]{2,1,0:T(8,128)(2,1)S(1)}, u32[]{:S(2)}, u32[]{:S(2)}) collective-permute-start(bf16[1,256,1792]{2,1,0:T(8,128)(2,1)S(1)} %copy-done.5), channel_id=1, source_target_pairs={{128,0},{256,128},{384,256},{0,384},{129,1},{257,129},{385,257},{1... | collective-permute-start | bytes 2752520 | tf_op jit(solution)/shard_map/ppermute | solution.py:19
  27.4 24.4 %collective-permute-start = (bf16[1,256,1792]{2,1,0:T(8,128)(2,1)S(1)}, bf16[1,256,1792]{2,1,0:T(8,128)(2,1)S(1)}, u32[]{:S(2)}, u32[]{:S(2)}) collective-permute-start(bf16[1,256,1792]{2,1,0:T(8,128)(2,1)S(1)} %copy-done.5), channel_id=1, source_target_pairs={{0,128},{128,256},{256,384},{384,0},{1,129},{129,257},{257,385},{3... | collective-permute-start | bytes 2752520 | tf_op jit(solution)/shard_map/ppermute | solution.py:16
  48.6 3.2 copy-start.6
  51.8 0.9 copy-start.7
  52.7 57.4 %copy-start = (bf16[1,256,1792]{2,1,0:T(8,128)(2,1)S(1)}, bf16[1,256,1792]{2,1,0:T(8,128)(2,1)}, u32[]{:S(2)}) copy-start(bf16[1,256,1792]{2,1,0:T(8,128)(2,1)} %param.7) | copy-start | bytes 2752516
  113.1 213.6 %all-reduce.6.cloned.1.call-start = ((), (), s32[]{:S(2)}) async-start(), calls=%async_computation.3 | async-start | bytes 2097152 | tf_op jit(solution)/shard_map/psum | solution.py:53
  188.4 380.2 %reduce-scatter.2.cloned.1.call-start = ((), (), s32[]{:S(2)}) async-start(), calls=%async_computation.4 | async-start | bytes 3899392 | tf_op jit(solution)/shard_map/reduce_scatter | solution.py:59
  331.1 1.0 copy-start.4
  395.1 86.8 %copy-start.1 = (f32[256,512]{1,0:T(8,128)S(1)}, f32[256,512]{1,0:T(8,128)}, u32[]{:S(2)}) copy-start(f32[256,512]{1,0:T(8,128)} %all-reduce.4.cloned.1.call-done) | copy-start | bytes 1572868
  488.2 3.0 copy-start.2
  493.6 90.3 %copy-start.3 = (f32[128,256]{1,0:T(8,128)S(1)}, f32[128,256]{1,0:T(8,128)}, u32[]{:S(2)}) copy-start(f32[128,256]{1,0:T(8,128)} %copy-done.2) | copy-start | bytes 393220
  493.6 159.2 %all-gather.2.cloned.1.call-start = ((), (), s32[]{:S(2)}) async-start(), calls=%async_computation.5 | async-start | bytes 1949696 | tf_op jit(solution)/shard_map/all_gather | solution.py:67
Sparse Core Ops, SparseCore 0:
  113.2 71.8 all-reduce.3
  188.6 138.1 all-reduce.5
  493.8 74.8 reduce-scatter.1
  584.1 68.6 all-gather.1
